TPU v7x, 32 devices: a whole 2x2x4 slice. The times are simulated.
32 devices in a mesh: rep: 2 (over core), shard: 16 (over z, y, x).
Axes of the slice: x: 2, y: 2, z: 4, core: 2. Of those that a mesh axis runs over, the one named last changes fastest.
Arguments:
- tokens: bfloat16 [32, 1024, 768], P('rep', 'shard'), may hold values from -6 to 6
- cotangent: bfloat16 [32, 1024, 768], P('rep', 'shard'), may hold values from -6 to 6
- lengths: int32 [2, 16], P('rep'), may hold values from 512 to 1024, as said below
- order: int32 [2, 16], P('rep'), may hold values from 0 to 15, each once within a row
- norm_weight: bfloat16 [768], P('shard'), may hold values from 0.099609375 to 1.8984375
- in_weight: bfloat16 [768, 3352], P('shard'), may hold values from -0.21875 to 0.21875
- conv_weight: bfloat16 [1792, 4], P('shard'), may hold values from -3 to 3
- conv_bias: bfloat16 [1792], P('shard'), may hold values from -3 to 3
- step_bias: float32 [24], replicated, may hold values from -5.5 to -2.5
- decay_log: float32 [24], replicated, may hold values from 0 to 2.77
- skip_gain: float32 [24], replicated, may hold values from 0.5 to 1.5
- gate_norm_weight: bfloat16 [1536], P('shard'), may hold values from 0.099609375 to 1.8984375
- out_weight: bfloat16 [1536, 768], P('shard'), may hold values from -0.15625 to 0.15625
Outputs:
- output: bfloat16 [32, 1024, 768], P('rep', 'shard')
- input_grad: bfloat16 [32, 1024, 768], P('rep', 'shard')
- grad_norm: float32 [768], P('shard')
- grad_in: float32 [768, 3352], P('shard')
- grad_conv: float32 [1792, 4], P('shard')
- grad_conv_bias: float32 [1792], P('shard')
- grad_step_bias: float32 [24], replicated
- grad_decay_log: float32 [24], replicated
- grad_skip: float32 [24], replicated
- grad_gate_norm: float32 [1536], P('shard')
- grad_out: float32 [1536, 768], P('shard')
Inputs may be any that keep to these rules, and one draw needn't show every extreme that they name: Each row of order holds every number from 0 to 15 once: slot k of group r holds sequence order[r, k]. lengths[r, s] counts the valid leading positions of sequence s of group r; each row has one entry equal to 1024 and one equal to 512.
All inputs are finite; a program needn't handle non-finite values.
Results may differ from a plain program's by a relative error of at most 0.012.
The roundings to bfloat16 on the way count: a program that leaves them out, or rounds other values in their place, can miss the bound.
Values may be sent and summed in bfloat16 or wider, within the bound.
A program may use at most 192 MiB of HBM per device.

v0:
```python
import jax
import jax.numpy as jnp
from jax import lax
from jax.sharding import PartitionSpec as P

HEADS = 24
HEADDIM = 64
STATE = 128
CONV = 4
SPAN = 256
DI = 1536
XBC = 1792
epsilon = 1e-05


def decay_terms(log_block, step_block):
    cumul = jnp.cumsum(log_block, axis=0)
    cumul_heads = cumul.T
    positions = log_block.shape[0]
    causal = jnp.arange(positions)[:, None] >= jnp.arange(positions)[None, :]
    spread = jnp.where(causal[None], cumul_heads[:, :, None] - cumul_heads[:, None, :], 0.0)
    factor = jnp.where(causal[None], jnp.exp(spread), 0.0) * step_block.T[:, None, :]
    carry_weight = jnp.exp(cumul[-1][None, :] - cumul) * step_block
    return (factor, carry_weight, jnp.exp(cumul), jnp.exp(cumul[-1]))


def norm_part(tok_float, norm_gain):
    return (
        tok_float
        * lax.rsqrt(jnp.mean(tok_float * tok_float, axis=-1, keepdims=True) + epsilon)
        * norm_gain
    )


def conv_part(conv_in, conv_taps, conv_shift):
    length = conv_in.shape[0]
    padded = jnp.concatenate(
        [jnp.zeros((CONV - 1, conv_in.shape[1]), jnp.float32), conv_in], axis=0
    )
    total = conv_shift[None, :] + jnp.zeros_like(conv_in)
    for tap in range(CONV):
        total = total + conv_taps[:, tap][None, :] * padded[tap : tap + length]
    return jax.nn.silu(total)


def step_part(step_raw, step_bias, decay_log):
    step_size = jax.nn.softplus(step_raw + step_bias[None, :])
    return (step_size, -jnp.exp(decay_log)[None, :] * step_size)


def gate_part(scan_out, heads_in, skip_gain, gate_raw, gate_gain):
    mixed = scan_out + jnp.repeat(skip_gain, HEADDIM)[None, :] * heads_in
    gated = mixed * jax.nn.silu(gate_raw)
    return gated * lax.rsqrt(jnp.mean(gated * gated, axis=-1, keepdims=True) + epsilon) * gate_gain


def block_forward(state, inputs):
    heads_blk, keys_blk, query_blk, step_blk, log_blk = inputs
    factor, carry_weight, growth, growth_last = decay_terms(log_blk, step_blk)
    scores = jnp.einsum("tn,sn->ts", query_blk, keys_blk, preferred_element_type=jnp.float32)
    mixing = (scores[None] * factor).astype(jnp.bfloat16)
    within = jnp.einsum("hts,shp->thp", mixing, heads_blk, preferred_element_type=jnp.float32)
    across = jnp.einsum(
        "tn,hpn->thp", query_blk, state.astype(jnp.bfloat16), preferred_element_type=jnp.float32
    )
    result = within + growth[:, :, None] * across
    weighted = (heads_blk.astype(jnp.float32) * carry_weight[:, :, None]).astype(jnp.bfloat16)
    contrib = jnp.einsum("sn,shp->hpn", keys_blk, weighted, preferred_element_type=jnp.float32)
    return (growth_last[:, None, None] * state + contrib, (result, state))


def block_backward(later, inputs):
    heads_blk, keys_blk, query_blk, step_blk, log_blk, grad_blk, state = inputs
    terms, decay_pull = jax.vjp(decay_terms, log_blk, step_blk)
    factor, carry_weight, growth, growth_last = terms
    scores = jnp.einsum("tn,sn->ts", query_blk, keys_blk, preferred_element_type=jnp.float32)
    mixing = (scores[None] * factor).astype(jnp.bfloat16)
    state_low = state.astype(jnp.bfloat16)
    across = jnp.einsum("tn,hpn->thp", query_blk, state_low, preferred_element_type=jnp.float32)
    heads_float = heads_blk.astype(jnp.float32)
    weighted = (heads_float * carry_weight[:, :, None]).astype(jnp.bfloat16)
    grad_within = grad_blk.astype(jnp.bfloat16)
    grad_across = (growth[:, :, None] * grad_blk).astype(jnp.bfloat16)
    grad_mixing = jnp.einsum(
        "thp,shp->hts", grad_within, heads_blk, preferred_element_type=jnp.float32
    )
    grad_heads = jnp.einsum("hts,thp->shp", mixing, grad_within, preferred_element_type=jnp.float32)
    grad_query = jnp.einsum(
        "thp,hpn->tn", grad_across, state_low, preferred_element_type=jnp.float32
    )
    grad_state = jnp.einsum(
        "thp,tn->hpn", grad_across, query_blk, preferred_element_type=jnp.float32
    )
    grad_state = grad_state + growth_last[:, None, None] * later
    grad_growth = jnp.sum(grad_blk * across, axis=2)
    later_low = later.astype(jnp.bfloat16)
    grad_weighted = jnp.einsum(
        "hpn,sn->shp", later_low, keys_blk, preferred_element_type=jnp.float32
    )
    grad_keys = jnp.einsum("hpn,shp->sn", later_low, weighted, preferred_element_type=jnp.float32)
    grad_heads = grad_heads + grad_weighted * carry_weight[:, :, None]
    grad_carry = jnp.sum(grad_weighted * heads_float, axis=2)
    grad_last = jnp.sum(later * state, axis=(1, 2))
    grad_scores = jnp.sum(grad_mixing * factor, axis=0).astype(jnp.bfloat16)
    grad_query = grad_query + jnp.dot(grad_scores, keys_blk, preferred_element_type=jnp.float32)
    grad_keys = grad_keys + jnp.einsum(
        "ts,tn->sn", grad_scores, query_blk, preferred_element_type=jnp.float32
    )
    grad_log, grad_step = decay_pull(
        (grad_mixing * scores[None], grad_carry, grad_growth, grad_last)
    )
    return (grad_state, (grad_heads, grad_keys, grad_query, grad_step, grad_log))


def forward_seq(
    tok_float,
    keep,
    norm_full,
    in_full,
    conv_full,
    shift_full,
    gate_full,
    out_full,
    step_bias,
    decay_log,
    skip_gain,
):
    seq_len = tok_float.shape[0]
    normed, norm_pull = jax.vjp(norm_part, tok_float, norm_full.astype(jnp.float32))
    normed_low = normed.astype(jnp.bfloat16)
    projected = jnp.dot(normed_low, in_full, preferred_element_type=jnp.float32)
    gate_raw = projected[:, :DI]
    conv_in = projected[:, DI : DI + XBC]
    step_raw = projected[:, DI + XBC :]
    convolved, conv_pull = jax.vjp(
        conv_part, conv_in, conv_full.astype(jnp.float32), shift_full.astype(jnp.float32)
    )
    heads_in = convolved[:, :DI]
    heads_low = heads_in.astype(jnp.bfloat16)
    key_low = convolved[:, DI : DI + STATE].astype(jnp.bfloat16)
    query_low = convolved[:, DI + STATE :].astype(jnp.bfloat16)
    decays, step_pull = jax.vjp(step_part, step_raw, step_bias, decay_log)
    step_size, log_decay = decays
    count = seq_len // SPAN
    blocks = (
        heads_low.reshape(count, SPAN, HEADS, HEADDIM),
        key_low.reshape(count, SPAN, STATE),
        query_low.reshape(count, SPAN, STATE),
        step_size.reshape(count, SPAN, HEADS),
        log_decay.reshape(count, SPAN, HEADS),
    )
    start = jnp.zeros((HEADS, HEADDIM, STATE), jnp.float32)
    final_state, kept = lax.scan(block_forward, start, blocks)
    scan_blocks, states = kept
    scan_out = scan_blocks.reshape(seq_len, DI)
    gate_value, gate_pull = jax.vjp(
        gate_part, scan_out, heads_in, skip_gain, gate_raw, gate_full.astype(jnp.float32)
    )
    gate_low = gate_value.astype(jnp.bfloat16)
    branch = jnp.dot(gate_low, out_full, preferred_element_type=jnp.float32)
    result = (tok_float + keep[:, None] * branch).astype(jnp.bfloat16)
    saved = (keep, normed_low, norm_pull, conv_pull, step_pull, gate_pull, gate_low, blocks, states)
    return (result, saved)


def backward_seq(saved, cot_float, in_full, out_full):
    keep, normed_low, norm_pull, conv_pull, step_pull, gate_pull, gate_low, blocks, states = saved
    seq_len = cot_float.shape[0]
    count = seq_len // SPAN
    grad_branch = (keep[:, None] * cot_float).astype(jnp.bfloat16)
    grad_out_full = jnp.einsum(
        "ti,tj->ij", gate_low, grad_branch, preferred_element_type=jnp.float32
    )
    grad_gate = jnp.einsum("tj,ij->ti", grad_branch, out_full, preferred_element_type=jnp.float32)
    grad_scan, grad_heads_skip, grad_skip, grad_gate_raw, grad_gate_gain = gate_pull(grad_gate)
    grad_scan_blocks = grad_scan.reshape(count, SPAN, HEADS, HEADDIM)
    first_grad, grads = lax.scan(
        block_backward,
        jnp.zeros((HEADS, HEADDIM, STATE), jnp.float32),
        (blocks[0], blocks[1], blocks[2], blocks[3], blocks[4], grad_scan_blocks, states),
        reverse=True,
    )
    grad_heads, grad_keys, grad_query, grad_step, grad_log = grads
    grad_step_raw, grad_step_bias, grad_decay_log = step_pull(
        (grad_step.reshape(seq_len, HEADS), grad_log.reshape(seq_len, HEADS))
    )
    grad_convolved = jnp.concatenate(
        [
            grad_heads.reshape(seq_len, DI) + grad_heads_skip,
            grad_keys.reshape(seq_len, STATE),
            grad_query.reshape(seq_len, STATE),
        ],
        axis=1,
    )
    grad_conv_in, grad_taps, grad_shift = conv_pull(grad_convolved)
    grad_projected = jnp.concatenate([grad_gate_raw, grad_conv_in, grad_step_raw], axis=1).astype(
        jnp.bfloat16
    )
    grad_in_full = jnp.einsum(
        "ti,tj->ij", normed_low, grad_projected, preferred_element_type=jnp.float32
    )
    grad_normed = jnp.einsum(
        "tj,ij->ti", grad_projected, in_full, preferred_element_type=jnp.float32
    )
    grad_tok, grad_norm_gain = norm_pull(grad_normed)
    input_grad = (cot_float + grad_tok).astype(jnp.bfloat16)
    weight_grads = (
        grad_norm_gain,
        grad_in_full,
        grad_taps,
        grad_shift,
        grad_gate_gain,
        grad_out_full,
    )
    return (input_grad, weight_grads, (grad_step_bias, grad_decay_log, grad_skip))


def on_device(
    tokens,
    cotangent,
    lengths,
    order,
    norm_weight,
    in_weight,
    conv_weight,
    conv_bias,
    step_bias,
    decay_log,
    skip_gain,
    gate_norm_weight,
    out_weight,
):
    peers = lax.axis_size("shard")
    rank = lax.axis_index("shard")
    slots = jnp.arange(peers, dtype=jnp.int32)
    order_row = order[0]
    inverse = jnp.sum(jnp.where(order_row[None, :] == slots[:, None], slots[None, :], 0), axis=1)
    piece = tokens.shape[1]
    width = tokens.shape[2]
    sent_tokens = jnp.take(tokens, inverse, axis=0).reshape(peers, 1, piece, width)
    sent_cot = jnp.take(cotangent, inverse, axis=0).reshape(peers, 1, piece, width)
    got_tokens, got_cot = (
        lax.all_to_all(sent_tokens, "shard", split_axis=0, concat_axis=2, tiled=True),
        lax.all_to_all(sent_cot, "shard", split_axis=0, concat_axis=2, tiled=True),
    )
    seq_len = got_tokens.shape[2]
    length_row = lengths[0]
    gathered = (
        lax.all_gather(norm_weight, "shard", axis=0, tiled=True),
        lax.all_gather(in_weight, "shard", axis=0, tiled=True),
        lax.all_gather(conv_weight, "shard", axis=0, tiled=True),
        lax.all_gather(conv_bias, "shard", axis=0, tiled=True),
        lax.all_gather(gate_norm_weight, "shard", axis=0, tiled=True),
        lax.all_gather(out_weight, "shard", axis=0, tiled=True),
    )
    norm_full, in_full, conv_full, shift_full, gate_full, out_full = gathered
    valid = length_row[rank]
    keep = (jnp.arange(seq_len, dtype=jnp.int32) < valid).astype(jnp.float32)
    forward_out, saved = forward_seq(
        got_tokens[0, 0].astype(jnp.float32),
        keep,
        norm_full,
        in_full,
        conv_full,
        shift_full,
        gate_full,
        out_full,
        step_bias,
        decay_log,
        skip_gain,
    )
    result = forward_out[None]
    grad_seq, weight_grads, head_terms = backward_seq(
        saved, got_cot[0, 0].astype(jnp.float32), in_full, out_full
    )
    input_grad = grad_seq[None]
    back_out, back_grad = (
        lax.all_to_all(result, "shard", split_axis=1, concat_axis=0, tiled=True),
        lax.all_to_all(input_grad, "shard", split_axis=1, concat_axis=0, tiled=True),
    )
    output = jnp.take(back_out, order_row, axis=0)
    input_back = jnp.take(back_grad, order_row, axis=0)
    summed = lax.psum(
        (
            weight_grads[0],
            weight_grads[1],
            weight_grads[2],
            weight_grads[3],
            weight_grads[4],
            weight_grads[5],
        ),
        "rep",
    )
    pieces = (
        lax.psum_scatter(summed[0], "shard", scatter_dimension=0, tiled=True),
        lax.psum_scatter(summed[1], "shard", scatter_dimension=0, tiled=True),
        lax.psum_scatter(summed[2], "shard", scatter_dimension=0, tiled=True),
        lax.psum_scatter(summed[3], "shard", scatter_dimension=0, tiled=True),
        lax.psum_scatter(summed[4], "shard", scatter_dimension=0, tiled=True),
        lax.psum_scatter(summed[5], "shard", scatter_dimension=0, tiled=True),
    )
    head_sums = lax.psum((head_terms[0], head_terms[1], head_terms[2]), ("rep", "shard"))
    return (
        output,
        input_back,
        pieces[0],
        pieces[1],
        pieces[2],
        pieces[3],
        head_sums[0],
        head_sums[1],
        head_sums[2],
        pieces[4],
        pieces[5],
    )


def solution(mesh):
    placed = (
        P("rep", "shard", None),
        P("rep", "shard", None),
        P("rep", None),
        P("rep", None),
        P("shard"),
        P("shard", None),
        P("shard", None),
        P("shard"),
        P(),
        P(),
        P(),
        P("shard"),
        P("shard", None),
    )
    return jax.shard_map(
        on_device,
        mesh=mesh,
        in_specs=placed,
        out_specs=(
            P("rep", "shard", None),
            P("rep", "shard", None),
            P("shard"),
            P("shard", None),
            P("shard", None),
            P("shard"),
            P(),
            P(),
            P(),
            P("shard"),
            P("shard", None),
        ),
        check_vma=False,
    )
```

profile of v0, /device:TPU:0, one launch (start us, length us, event | category | flops | bytes accessed | tf_op | source)
XLA Modules:
  0.0 1286.4 jit_solution(3603219273039151114)
XLA Ops:
  15.6 65.5 %all_to_all.42 = bf16[16,1,64,768]{3,2,1,0:T(8,128)(2,1)S(1)} all-to-all(bf16[16,1,64,768]{3,2,1,0:T(8,128)(2,1)S(1)} %get-tuple-element.698), channel_id=1, replica_groups=mesh['rep'=2,'shard'=16] {'shard'}, dimensions={0} | all-to-all | bytes 3145728 | tf_op jit(solution)/shard_map/all_to_all | solution.py:243
  89.8 115.9 %all-reduce.21 = (bf16[768]{0:T(1024)(128)(2,1)S(1)}, bf16[1792]{0:T(1024)(128)(2,1)S(1)}, bf16[1536]{0:T(1024)(128)(2,1)S(1)}) all-reduce(bf16[768]{0:T(1024)(128)(2,1)S(1)} %dynamic-update-slice, bf16[1792]{0:T(1024)(128)(2,1)S(1)} %dynamic-update-slice.1, ...), channel_id=1, replica_groups=mesh['rep'=2,'shard'=16] {'shard'}, use_global_device_ids=true, to_apply=%add.11 | all-reduce | flops 4096 | bytes 16384
  205.8 35.7 %all-gather = bf16[16,112,4]{1,2,0:T(4,128)(2,1)S(1)} all-gather(bf16[1,112,4]{1,2,0:T(4,128)(2,1)S(1)} %bitcast.455), channel_id=1, replica_groups=mesh['rep'=2,'shard'=16] {'shard'}, dimensions={0}, use_global_device_ids=true | all-gather | bytes 15232 | tf_op jit(solution)/shard_map/all_gather | solution.py:251
  297.2 182.0 %while.40 = (s32[]{:T(128)}, f32[24,64,128]{2,1,0:T(8,128)S(1)}, f32[4,256,24,64]{1,0,3,2:T(4,128)}, f32[4,24,64,128]{3,2,1,0:T(8,128)}, f32[4,256,24]{1,2,0:T(8...) while((s32[]{:T(128)}, f32[24,64,128]{2,1,0:T(8,128)S(1)}, ...), condition=%wide.region_5.7_spmd.clone, body=%wide.region_2.0_spmd.clone.sunk | while | flops 432687168 | bytes 17880888 | solution.py:153
  305.7 34.5 %dynamic_update_slice.73 = f32[4,256,24,64]{1,0,3,2:T(4,128)} dynamic-update-slice(f32[4,256,24,64]{1,0,3,2:T(4,128)} %get-tuple-element.896, f32[1,256,24,64]{1,0,3,2:T(1,128)S(1)} %copy.355, s32[]{:T(128)} %get-tuple-element.894, s32[]{:T(128)} %constant.126.clone.1..sunk, s32[]{:T(128)} %constant.126.clone.1..sunk, s32[]{:T(128)} %constant.126.clone.1..sunk) | dynamic-update-slice | bytes 3145732 | tf_op jit(solution)/shard_map/while/body/jit(dynamic_update_index_in_dim)/dynamic_update_slice | solution.py:153
  351.2 34.5 %dynamic_update_slice.73 = f32[4,256,24,64]{1,0,3,2:T(4,128)} dynamic-update-slice(f32[4,256,24,64]{1,0,3,2:T(4,128)} %get-tuple-element.896, f32[1,256,24,64]{1,0,3,2:T(1,128)S(1)} %copy.355, s32[]{:T(128)} %get-tuple-element.894, s32[]{:T(128)} %constant.126.clone.1..sunk, s32[]{:T(128)} %constant.126.clone.1..sunk, s32[]{:T(128)} %constant.126.clone.1..sunk) | dynamic-update-slice | bytes 3145732 | tf_op jit(solution)/shard_map/while/body/jit(dynamic_update_index_in_dim)/dynamic_update_slice | solution.py:153
  396.6 34.5 %dynamic_update_slice.73 = f32[4,256,24,64]{1,0,3,2:T(4,128)} dynamic-update-slice(f32[4,256,24,64]{1,0,3,2:T(4,128)} %get-tuple-element.896, f32[1,256,24,64]{1,0,3,2:T(1,128)S(1)} %copy.355, s32[]{:T(128)} %get-tuple-element.894, s32[]{:T(128)} %constant.126.clone.1..sunk, s32[]{:T(128)} %constant.126.clone.1..sunk, s32[]{:T(128)} %constant.126.clone.1..sunk) | dynamic-update-slice | bytes 3145732 | tf_op jit(solution)/shard_map/while/body/jit(dynamic_update_index_in_dim)/dynamic_update_slice | solution.py:153
  442.1 34.5 %dynamic_update_slice.73 = f32[4,256,24,64]{1,0,3,2:T(4,128)} dynamic-update-slice(f32[4,256,24,64]{1,0,3,2:T(4,128)} %get-tuple-element.896, f32[1,256,24,64]{1,0,3,2:T(1,128)S(1)} %copy.355, s32[]{:T(128)} %get-tuple-element.894, s32[]{:T(128)} %constant.126.clone.1..sunk, s32[]{:T(128)} %constant.126.clone.1..sunk, s32[]{:T(128)} %constant.126.clone.1..sunk) | dynamic-update-slice | bytes 3145732 | tf_op jit(solution)/shard_map/while/body/jit(dynamic_update_index_in_dim)/dynamic_update_slice | solution.py:153
  506.9 14.3 %multiply_reduce_fusion.7 = (f32[1536]{0:T(1024)}, f32[1024,1536]{0,1:T(8,128)}, bf16[1024,1536]{0,1:T(8,128)(2,1)}) fusion(f32[1024,1792]{0,1:T(8,128)} %copy-done.2, f32[1024,3352]{0,1:T(8,128)} %fusion.140, f32[1024,1536]{0,1:T(8,128)S(1)} %copy-done.8, f32[1024]{0:T(1024)S(1)} %multiply_multiply_fusion.1, f32[1024]{0:T(1024)S(1)} %fusion.127, ...), kind=kLoop, calls=%fused_computation.179 | loop fusion | flops 34601472 | bytes 40921088 | tf_op jit(solution)/shard_map/transpose(jvp())/reduce_sum | solution.py:52
  536.4 292.3 %while.41 = (s32[]{:T(128)}, f32[24,64,128]{2,1,0:T(8,128)S(1)}, f32[4,256,24,64]{1,0,3,2:T(4,128)}, f32[4,256,128]{2,1,0:T(8,128)}, f32[4,256,128]{2,1,0:T(8,12...) while((s32[]{:T(128)}, f32[24,64,128]{2,1,0:T(8,128)S(1)}, ...), condition=%wide.region_21.23_spmd.clone, body=%wide.region_8.22_spmd.clone.sunk | while | flops 998139968 | bytes 33770432 | solution.py:177
  562.6 34.8 %dynamic_update_slice.76 = f32[4,256,24,64]{1,0,3,2:T(4,128)} dynamic-update-slice(f32[4,256,24,64]{1,0,3,2:T(4,128)} %get-tuple-element.938, f32[1,256,24,64]{1,0,3,2:T(1,128)} %copy.368, s32[]{:T(128)S(6)} %sub.232, s32[]{:T(128)} %constant.126.clone.1..sunk.1, s32[]{:T(128)} %constant.126.clone.1..sunk.1, s32[]{:T(128)} %constant.126.clone.1..sunk.1) | dynamic-update-slice | bytes 3145732 | tf_op jit(solution)/shard_map/while/body/jit(dynamic_update_index_in_dim)/dynamic_update_slice | solution.py:153
  635.7 34.7 %dynamic_update_slice.76 = f32[4,256,24,64]{1,0,3,2:T(4,128)} dynamic-update-slice(f32[4,256,24,64]{1,0,3,2:T(4,128)} %get-tuple-element.938, f32[1,256,24,64]{1,0,3,2:T(1,128)} %copy.368, s32[]{:T(128)S(6)} %sub.232, s32[]{:T(128)} %constant.126.clone.1..sunk.1, s32[]{:T(128)} %constant.126.clone.1..sunk.1, s32[]{:T(128)} %constant.126.clone.1..sunk.1) | dynamic-update-slice | bytes 3145732 | tf_op jit(solution)/shard_map/while/body/jit(dynamic_update_index_in_dim)/dynamic_update_slice | solution.py:153
  708.7 34.7 %dynamic_update_slice.76 = f32[4,256,24,64]{1,0,3,2:T(4,128)} dynamic-update-slice(f32[4,256,24,64]{1,0,3,2:T(4,128)} %get-tuple-element.938, f32[1,256,24,64]{1,0,3,2:T(1,128)} %copy.368, s32[]{:T(128)S(6)} %sub.232, s32[]{:T(128)} %constant.126.clone.1..sunk.1, s32[]{:T(128)} %constant.126.clone.1..sunk.1, s32[]{:T(128)} %constant.126.clone.1..sunk.1) | dynamic-update-slice | bytes 3145732 | tf_op jit(solution)/shard_map/while/body/jit(dynamic_update_index_in_dim)/dynamic_update_slice | solution.py:153
  781.7 34.7 %dynamic_update_slice.76 = f32[4,256,24,64]{1,0,3,2:T(4,128)} dynamic-update-slice(f32[4,256,24,64]{1,0,3,2:T(4,128)} %get-tuple-element.938, f32[1,256,24,64]{1,0,3,2:T(1,128)} %copy.368, s32[]{:T(128)S(6)} %sub.232, s32[]{:T(128)} %constant.126.clone.1..sunk.1, s32[]{:T(128)} %constant.126.clone.1..sunk.1, s32[]{:T(128)} %constant.126.clone.1..sunk.1) | dynamic-update-slice | bytes 3145732 | tf_op jit(solution)/shard_map/while/body/jit(dynamic_update_index_in_dim)/dynamic_update_slice | solution.py:153
  844.6 19.0 %multiply_reduce_fusion.4 = (f32[1792]{0:T(1024)S(1)}, f32[1792]{0:T(1024)S(1)}, f32[1792]{0:T(1024)S(1)}, f32[1792]{0:T(1024)S(1)}, f32[1792]{0:T(1024)S(1)}, /*index=5*/f32[1024,1792]{0,1:T(8,128)S(1)}) fusion(f32[1024,1792]{0,1:T(8,128)} %copy-done.3, f32[1024,3352]{0,1:T(8,128)} %fusion.140, f32[1024,1792]{0,1:T(8,128)} %get-tuple-element.668, ...), kind=kLoop, calls=%fused_computation.169 | loop fusion | flops 36691200 | bytes 36736000 | tf_op jit(solution)/shard_map/transpose(jvp())/reduce_sum | solution.py:42
  872.1 12.1 fusion.103
  884.3 12.9 %fusion.119 = f32[768,3352]{1,0:T(8,128)} fusion(bf16[1024,768]{1,0:T(8,128)(2,1)S(1)} %copy-done.11, bf16[1024,24]{0,1:T(8,128)(2,1)S(1)} %get-tuple-element.662, bf16[1024,1792]{0,1:T(8,128)(2,1)} %fusion.103, bf16[1024,1536]{0,1:T(8,128)(2,1)} %get-tuple-element.685), kind=kOutput, calls=%fused_computation.210 | convolution fusion | flops 5292834816 | bytes 18735104 | tf_op jit(solution)/shard_map/ti,tj->ij/dot_general | solution.py:199
  909.6 11.7 reduce.22
  943.6 11.5 reduce.21
  956.5 20.8 %all-to-all-done.1 = bf16[16,2,24576]{2,1,0:T(2,128)(2,1)S(1)} async-done(((bf16[16,2,24576]{2,1,0:T(2,128)(2,1)}), bf16[16,2,24576]{2,1,0:T(2,128)(2,1)S(1)}, u32[]{:S(2)}, u32[]{:S(2)}) %all-to-all-start.1) | async-done | bytes 1572896 | tf_op jit(solution)/shard_map/all_to_all | solution.py:278
  977.2 27.4 %all-to-all-start.3 = ((bf16[16,2,24576]{2,1,0:T(2,128)(2,1)}), bf16[16,2,24576]{2,1,0:T(2,128)(2,1)S(1)}, u32[]{:S(2)}, u32[]{:S(2)}) async-start(bf16[16,2,24576]{2,1,0:T(2,128)(2,1)} %reshape.519), calls=%async_computation.3 | async-start | bytes 3145728 | tf_op jit(solution)/shard_map/all_to_all | solution.py:279
  1008.1 122.2 %reduce-scatter.6.cloned.1.call-done = f32[48,3352]{1,0:T(8,128)} async-done(((f32[768,3352]{1,0:T(8,128)}), f32[48,3352]{1,0:T(8,128)}) %reduce-scatter.6.cloned.1.call-update) | async-done | bytes 643600 | tf_op jit(solution)/shard_map/reduce_scatter | solution.py:296
  1130.6 40.0 %all-reduce.17 = (f32[24]{0:T(128)}, f32[24]{0:T(128)}, f32[24]{0:T(128)}) all-reduce(f32[24]{0:T(128)S(1)} %get-tuple-element.661, f32[24]{0:T(128)S(1)} %negate_multiply_fusion, f32[24]{0:T(128)S(1)} %reduce_sum.344), channel_id=1, replica_groups=mesh['rep'=2,'shard'=16] {'rep','shard'}, use_global_device_ids=true, to_apply=%region_38.40 | all-reduce | flops 72 | bytes 576 | tf_op jit(solution)/shard_map/psum | solution.py:302
  1170.6 75.7 %all-reduce.18 = (f32[768]{0:T(1024)S(1)}, f32[1792]{0:T(1024)S(1)}, f32[1536]{0:T(1024)S(1)}) all-reduce(f32[768]{0:T(1024)S(1)} %get-tuple-element.592, f32[1792]{0:T(1024)S(1)} %get-tuple-element.590, f32[1536]{0:T(1024)S(1)} %copy-done.36), channel_id=2, replica_groups=mesh['rep'=2,'shard'=16] {'shard'}, use_global_device_ids=true, to_apply=%region_25.27.clone | all-reduce | flops 4096 | bytes 32768
  (440 shorter events, 404.4 us)
Async XLA Ops:
  7.2 240.9 %all-gather.4.cloned.1.call-start = ((), (), s32[]{:S(2)}) async-start(), calls=%async_computation.7 | async-start | bytes 5640192 | tf_op jit(solution)/shard_map/all_gather | solution.py:250
  12.6 73.9 %copy-start.41 = (u32[32]{0:T(128)S(1)}, u32[32]{0:T(128)}, u32[]{:S(2)}) copy-start(u32[32]{0:T(128)} %constant.162) | copy-start | bytes 388
  12.6 76.5 %copy-start.44 = (bf16[112]{0:T(256)(128)(2,1)S(1)}, bf16[112]{0:T(256)(128)(2,1)}, u32[]{:S(2)}) copy-start(bf16[112]{0:T(256)(128)(2,1)} %param.26) | copy-start | bytes 676
  12.6 76.7 %copy-start.45 = (bf16[96]{0:T(256)(128)(2,1)S(1)}, bf16[96]{0:T(256)(128)(2,1)}, u32[]{:S(2)}) copy-start(bf16[96]{0:T(256)(128)(2,1)} %param.30) | copy-start | bytes 580
  12.6 77.0 %copy-start.46 = (bf16[48]{0:T(256)(128)(2,1)S(1)}, bf16[48]{0:T(256)(128)(2,1)}, u32[]{:S(2)}) copy-start(bf16[48]{0:T(256)(128)(2,1)} %param.23) | copy-start | bytes 292
  12.6 193.1 %copy-start.42 = (bf16[112,4]{0,1:T(4,128)(2,1)S(1)}, bf16[112,4]{0,1:T(4,128)(2,1)}, u32[]{:S(2)}) copy-start(bf16[112,4]{0,1:T(4,128)(2,1)} %param.25) | copy-start | bytes 2692
  12.6 228.9 %copy-start.43 = (f32[24]{0:T(128)S(1)}, f32[24]{0:T(128)}, u32[]{:S(2)}) copy-start(f32[24]{0:T(128)} %param.29) | copy-start | bytes 292
  12.7 229.0 %copy-start.47 = (s32[1,16]{1,0:T(1,128)S(1)}, s32[1,16]{1,0:T(1,128)}, u32[]{:S(2)}) copy-start(s32[1,16]{1,0:T(1,128)} %param.21) | copy-start | bytes 196
  12.7 230.4 %copy-start.49 = (f32[24]{0:T(128)S(1)}, f32[24]{0:T(128)}, u32[]{:S(2)}) copy-start(f32[24]{0:T(128)} %param.28) | copy-start | bytes 292
  81.1 178.3 %copy-start.5 = (bf16[16,1,64,768]{3,2,1,0:T(8,128)(2,1)}, bf16[16,1,64,768]{3,2,1,0:T(8,128)(2,1)S(1)}, u32[]{:S(2)}) copy-start(bf16[16,1,64,768]{3,2,1,0:T(8,128)(2,1)S(1)} %all_to_all.42) | copy-start | bytes 4718596
  81.1 164.1 %all-to-all-start.2 = ((bf16[16,1,64,768]{3,2,1,0:T(8,128)(2,1)}), bf16[16,1,64,768]{3,2,1,0:T(8,128)(2,1)}, u32[]{:S(2)}, u32[]{:S(2)}) async-start(bf16[16,1,64,768]{3,2,1,0:T(8,128)(2,1)} %get-tuple-element.697), calls=%async_computation.2 | async-start | bytes 3145728 | tf_op jit(solution)/shard_map/all_to_all | solution.py:244
  85.6 413.4 %all-gather.6.cloned.1.call-start = ((), (), s32[]{:S(2)}) async-start(), calls=%async_computation.8 | async-start | bytes 2506752 | tf_op jit(solution)/shard_map/all_gather | solution.py:254
  86.4 921.7 %reduce-scatter.8.cloned.1.call-start = ((), (), s32[]{:S(2)}) async-start(), calls=%async_computation.10 | async-start | bytes 5013504 | tf_op jit(solution)/shard_map/reduce_scatter | solution.py:300
  205.8 53.7 %copy-start.23 = (f32[768]{0:T(1024)}, f32[768]{0:T(1024)S(1)}, u32[]{:S(2)}) copy-start(f32[768]{0:T(1024)S(1)} %convert_element_type.160) | copy-start | bytes 9220
  241.7 265.1 %copy-start.29 = (f32[1536]{0:T(1024)}, f32[1536]{0:T(1024)S(1)}, u32[]{:S(2)}) copy-start(f32[1536]{0:T(1024)S(1)} %convert_element_type.165) | copy-start | bytes 18436
  529.3 601.0 %reduce-scatter.6.cloned.1.call-start = ((), (), s32[]{:S(2)}) async-start(), calls=%async_computation.9 | async-start | bytes 11280384 | tf_op jit(solution)/shard_map/reduce_scatter | solution.py:296
  922.6 54.6 %all-to-all-start.1 = ((bf16[16,2,24576]{2,1,0:T(2,128)(2,1)}), bf16[16,2,24576]{2,1,0:T(2,128)(2,1)S(1)}, u32[]{:S(2)}, u32[]{:S(2)}) async-start(bf16[16,2,24576]{2,1,0:T(2,128)(2,1)} %reshape.517), calls=%async_computation.1 | async-start | bytes 3145728 | tf_op jit(solution)/shard_map/all_to_all | solution.py:278
  943.6 62.5 %copy-start.48 = (s32[1,16]{1,0:T(1,128)S(1)}, s32[1,16]{1,0:T(1,128)}, u32[]{:S(2)}) copy-start(s32[1,16]{1,0:T(1,128)} %param.22) | copy-start | bytes 196
  943.6 186.8 %copy-start.31 = (f32[1536]{0:T(1024)S(1)}, f32[1536]{0:T(1024)}, u32[]{:S(2)}) copy-start(f32[1536]{0:T(1024)} %get-tuple-element.659) | copy-start | bytes 18436
  943.6 187.0 %copy-start.50 = (f32[24]{0:T(128)S(1)}, f32[24]{0:T(128)}, u32[]{:S(2)}) copy-start(f32[24]{0:T(128)} %param.28) | copy-start | bytes 292
  943.6 227.0 %copy-start.36 = (f32[1536]{0:T(1024)S(1)}, f32[1536]{0:T(1024)}, u32[]{:S(2)}) copy-start(f32[1536]{0:T(1024)} %get-tuple-element.588) | copy-start | bytes 18436
  977.2 281.6 %all-to-all-start.3 = ((bf16[16,2,24576]{2,1,0:T(2,128)(2,1)}), bf16[16,2,24576]{2,1,0:T(2,128)(2,1)S(1)}, u32[]{:S(2)}, u32[]{:S(2)}) async-start(bf16[16,2,24576]{2,1,0:T(2,128)(2,1)} %reshape.519), calls=%async_computation.3 | async-start | bytes 3145728 | tf_op jit(solution)/shard_map/all_to_all | solution.py:279
  1004.6 241.9 %reduce-scatter.10.cloned.1.call-start = ((), (), s32[]{:S(2)}) async-start(), calls=%async_computation.11 | async-start | bytes 974848
  1006.1 269.6 %all-reduce.24.cloned.1.call-start = ((), (), s32[]{:S(2)}) async-start(), calls=%async_computation.12 | async-start | bytes 1916928 | tf_op jit(solution)/shard_map/psum | solution.py:283
  (36 other events, 436.0 us)
Sparse Core Ops, SparseCore 0:
  10.8 132.4 all-gather.3
  146.1 62.0 all-gather.5
  529.4 135.1 reduce-scatter.7
  897.3 232.9 reduce-scatter.5
  1133.0 76.8 reduce-scatter.9
  1212.3 15.8 all-reduce.23
where the time goes:
time: 1300 us; the launch traced here: 1290 us
  local copies, waits for them, and re-layouts  440 us (34%)
  blocking collectives  336 us (26%)
  matrix products  164 us (13%)
  other arithmetic  146 us (11%)
  waiting for transfers between devices  144 us (11%)
  starting transfers between devices  35.8 us (3%)
  between operations  19.1 us (1%)
    dynamic_update_slice x16, local copies, waits for them, and re-layouts, forward_seq(): final_state, kept = lax.scan(block_forward, start, blocks)  295 us
    unnamed x2, blocking collectives  192 us
    reduce_scatter x1, waiting for transfers between devices, on_device(): lax.psum_scatter(summed[1], 'shard', scatter_dimension=0, tiled=True)  122 us
    all_to_all x1, blocking collectives, on_device(): lax.all_to_all(sent_tokens, 'shard', split_axis=0, concat_axis=2, tiled=T...  65.5 us
    unnamed x131, local copies, waits for them, and re-layouts  55.2 us
    psum x1, blocking collectives, on_device(): lax.psum((head_terms[0], head_terms[1], head_terms[2]), ('rep', 'shard'))  40 us
    another operation x34, other arithmetic  37.8 us
    all_gather x1, blocking collectives, on_device(): lax.all_gather(conv_weight, 'shard', axis=0, tiled=True)  35.7 us
  transfers between devices with their start and end apart: 9, of which 2 were waited for; matrix products, arithmetic and copies ran while one was open for 55% of the time, Pallas kernels for 0%

commit v1 on v0

--- a/solution.py
+++ b/solution.py
@@ -299,7 +299,8 @@
         lax.psum_scatter(summed[4], "shard", scatter_dimension=0, tiled=True),
         lax.psum_scatter(summed[5], "shard", scatter_dimension=0, tiled=True),
     )
-    head_sums = lax.psum((head_terms[0], head_terms[1], head_terms[2]), ("rep", "shard"))
+    inner = lax.psum((head_terms[0], head_terms[1], head_terms[2]), "shard")
+    head_sums = lax.psum(inner, "rep")
     return (
         output,
         input_back,

time: 1300 us -> 1260 us (0.969)
  blocking collectives: 336 us -> 295 us
    psum x1 -> x0, blocking collectives: 40 us -> none  [on_device(): lax.psum((head_terms[0], head_terms[1], head_terms[2]), ('rep', 'shard'))]
    unnamed x131 -> x135, local copies, waits for them, and re-layouts: 55.2 us -> 53.4 us
  transfers between devices with their start and end apart: 9 -> 9, of which waited for: 2 -> 3; matrix products, arithmetic and copies ran while one was open for 55% -> 57% of each run, Pallas kernels for 0% -> 0%
where the time goes in v1:
time: 1260 us; the launch traced here: 1250 us
  local copies, waits for them, and re-layouts  439 us (35%)
  blocking collectives  295 us (23%)
  matrix products  164 us (13%)
  waiting for transfers between devices  148 us (12%)
  other arithmetic  146 us (12%)
  starting transfers between devices  35.8 us (3%)
  between operations  19.2 us (2%)
    dynamic_update_slice x16, local copies, waits for them, and re-layouts, forward_seq(): final_state, kept = lax.scan(block_forward, start, blocks)  295 us
    unnamed x2, blocking collectives  191 us
    reduce_scatter x1, waiting for transfers between devices, on_device(): lax.psum_scatter(summed[1], 'shard', scatter_dimension=0, tiled=True)  122 us
    all_to_all x1, blocking collectives, on_device(): lax.all_to_all(sent_tokens, 'shard', split_axis=0, concat_axis=2, tiled=T...  65.5 us
    unnamed x135, local copies, waits for them, and re-layouts  53.4 us
    another operation x34, other arithmetic  37.8 us
    all_gather x1, blocking collectives, on_device(): lax.all_gather(conv_weight, 'shard', axis=0, tiled=True)  35.7 us
    all_to_all x1, starting transfers between devices, on_device(): lax.all_to_all(input_grad, 'shard', split_axis=1, concat_axis=0, tiled=True)  27.4 us
  transfers between devices with their start and end apart: 9, of which 3 were waited for; matrix products, arithmetic and copies ran while one was open for 57% of the time, Pallas kernels for 0%

profile of v1, /device:TPU:0, one launch (start us, length us, event | category | flops | bytes accessed | tf_op | source)
XLA Modules:
  0.0 1248.1 jit_solution(8299810193421568275)
XLA Ops:
  15.6 65.5 %all_to_all.42 = bf16[16,1,64,768]{3,2,1,0:T(8,128)(2,1)S(1)} all-to-all(bf16[16,1,64,768]{3,2,1,0:T(8,128)(2,1)S(1)} %get-tuple-element.701), channel_id=1, replica_groups=mesh['rep'=2,'shard'=16] {'shard'}, dimensions={0} | all-to-all | bytes 3145728 | tf_op jit(solution)/shard_map/all_to_all | solution.py:243
  89.8 115.9 %all-reduce.20 = (bf16[768]{0:T(1024)(128)(2,1)S(1)}, bf16[1792]{0:T(1024)(128)(2,1)S(1)}, bf16[1536]{0:T(1024)(128)(2,1)S(1)}) all-reduce(bf16[768]{0:T(1024)(128)(2,1)S(1)} %dynamic-update-slice, bf16[1792]{0:T(1024)(128)(2,1)S(1)} %dynamic-update-slice.1, ...), channel_id=1, replica_groups=mesh['rep'=2,'shard'=16] {'shard'}, use_global_device_ids=true, to_apply=%add.11 | all-reduce | flops 4096 | bytes 16384
  205.8 35.7 %all-gather = bf16[16,112,4]{1,2,0:T(4,128)(2,1)S(1)} all-gather(bf16[1,112,4]{1,2,0:T(4,128)(2,1)S(1)} %bitcast.455), channel_id=1, replica_groups=mesh['rep'=2,'shard'=16] {'shard'}, dimensions={0}, use_global_device_ids=true | all-gather | bytes 15232 | tf_op jit(solution)/shard_map/all_gather | solution.py:251
  248.1 11.4 fusion.140
  297.2 182.0 %while.40 = (s32[]{:T(128)}, f32[24,64,128]{2,1,0:T(8,128)S(1)}, f32[4,256,24,64]{1,0,3,2:T(4,128)}, f32[4,24,64,128]{3,2,1,0:T(8,128)}, f32[4,256,24]{1,2,0:T(8...) while((s32[]{:T(128)}, f32[24,64,128]{2,1,0:T(8,128)S(1)}, ...), condition=%wide.region_5.7_spmd.clone, body=%wide.region_2.0_spmd.clone.sunk | while | flops 432687168 | bytes 17880888 | solution.py:153
  305.7 34.5 %dynamic_update_slice.73 = f32[4,256,24,64]{1,0,3,2:T(4,128)} dynamic-update-slice(f32[4,256,24,64]{1,0,3,2:T(4,128)} %get-tuple-element.899, f32[1,256,24,64]{1,0,3,2:T(1,128)S(1)} %copy.355, s32[]{:T(128)} %get-tuple-element.897, s32[]{:T(128)} %constant.126.clone.1..sunk, s32[]{:T(128)} %constant.126.clone.1..sunk, s32[]{:T(128)} %constant.126.clone.1..sunk) | dynamic-update-slice | bytes 3145732 | tf_op jit(solution)/shard_map/while/body/jit(dynamic_update_index_in_dim)/dynamic_update_slice | solution.py:153
  351.2 34.5 %dynamic_update_slice.73 = f32[4,256,24,64]{1,0,3,2:T(4,128)} dynamic-update-slice(f32[4,256,24,64]{1,0,3,2:T(4,128)} %get-tuple-element.899, f32[1,256,24,64]{1,0,3,2:T(1,128)S(1)} %copy.355, s32[]{:T(128)} %get-tuple-element.897, s32[]{:T(128)} %constant.126.clone.1..sunk, s32[]{:T(128)} %constant.126.clone.1..sunk, s32[]{:T(128)} %constant.126.clone.1..sunk) | dynamic-update-slice | bytes 3145732 | tf_op jit(solution)/shard_map/while/body/jit(dynamic_update_index_in_dim)/dynamic_update_slice | solution.py:153
  396.6 34.5 %dynamic_update_slice.73 = f32[4,256,24,64]{1,0,3,2:T(4,128)} dynamic-update-slice(f32[4,256,24,64]{1,0,3,2:T(4,128)} %get-tuple-element.899, f32[1,256,24,64]{1,0,3,2:T(1,128)S(1)} %copy.355, s32[]{:T(128)} %get-tuple-element.897, s32[]{:T(128)} %constant.126.clone.1..sunk, s32[]{:T(128)} %constant.126.clone.1..sunk, s32[]{:T(128)} %constant.126.clone.1..sunk) | dynamic-update-slice | bytes 3145732 | tf_op jit(solution)/shard_map/while/body/jit(dynamic_update_index_in_dim)/dynamic_update_slice | solution.py:153
  442.1 34.5 %dynamic_update_slice.73 = f32[4,256,24,64]{1,0,3,2:T(4,128)} dynamic-update-slice(f32[4,256,24,64]{1,0,3,2:T(4,128)} %get-tuple-element.899, f32[1,256,24,64]{1,0,3,2:T(1,128)S(1)} %copy.355, s32[]{:T(128)} %get-tuple-element.897, s32[]{:T(128)} %constant.126.clone.1..sunk, s32[]{:T(128)} %constant.126.clone.1..sunk, s32[]{:T(128)} %constant.126.clone.1..sunk) | dynamic-update-slice | bytes 3145732 | tf_op jit(solution)/shard_map/while/body/jit(dynamic_update_index_in_dim)/dynamic_update_slice | solution.py:153
  506.9 14.3 %multiply_reduce_fusion.7 = (f32[1536]{0:T(1024)}, f32[1024,1536]{0,1:T(8,128)}, bf16[1024,1536]{0,1:T(8,128)(2,1)}) fusion(f32[1024,1792]{0,1:T(8,128)} %copy-done.2, f32[1024,3352]{0,1:T(8,128)} %fusion.140, f32[1024,1536]{0,1:T(8,128)S(1)} %copy-done.8, f32[1024]{0:T(1024)S(1)} %multiply_multiply_fusion.1, f32[1024]{0:T(1024)S(1)} %fusion.127, ...), kind=kLoop, calls=%fused_computation.179 | loop fusion | flops 34601472 | bytes 40921088 | tf_op jit(solution)/shard_map/transpose(jvp())/reduce_sum | solution.py:52
  536.4 292.3 %while.41 = (s32[]{:T(128)}, f32[24,64,128]{2,1,0:T(8,128)S(1)}, f32[4,256,24,64]{1,0,3,2:T(4,128)}, f32[4,256,128]{2,1,0:T(8,128)}, f32[4,256,128]{2,1,0:T(8,12...) while((s32[]{:T(128)}, f32[24,64,128]{2,1,0:T(8,128)S(1)}, ...), condition=%wide.region_21.23_spmd.clone, body=%wide.region_8.22_spmd.clone.sunk | while | flops 998139968 | bytes 33770432 | solution.py:177
  562.6 34.8 %dynamic_update_slice.76 = f32[4,256,24,64]{1,0,3,2:T(4,128)} dynamic-update-slice(f32[4,256,24,64]{1,0,3,2:T(4,128)} %get-tuple-element.941, f32[1,256,24,64]{1,0,3,2:T(1,128)} %copy.368, s32[]{:T(128)S(6)} %sub.232, s32[]{:T(128)} %constant.126.clone.1..sunk.1, s32[]{:T(128)} %constant.126.clone.1..sunk.1, s32[]{:T(128)} %constant.126.clone.1..sunk.1) | dynamic-update-slice | bytes 3145732 | tf_op jit(solution)/shard_map/while/body/jit(dynamic_update_index_in_dim)/dynamic_update_slice | solution.py:153
  635.7 34.7 %dynamic_update_slice.76 = f32[4,256,24,64]{1,0,3,2:T(4,128)} dynamic-update-slice(f32[4,256,24,64]{1,0,3,2:T(4,128)} %get-tuple-element.941, f32[1,256,24,64]{1,0,3,2:T(1,128)} %copy.368, s32[]{:T(128)S(6)} %sub.232, s32[]{:T(128)} %constant.126.clone.1..sunk.1, s32[]{:T(128)} %constant.126.clone.1..sunk.1, s32[]{:T(128)} %constant.126.clone.1..sunk.1) | dynamic-update-slice | bytes 3145732 | tf_op jit(solution)/shard_map/while/body/jit(dynamic_update_index_in_dim)/dynamic_update_slice | solution.py:153
  708.7 34.7 %dynamic_update_slice.76 = f32[4,256,24,64]{1,0,3,2:T(4,128)} dynamic-update-slice(f32[4,256,24,64]{1,0,3,2:T(4,128)} %get-tuple-element.941, f32[1,256,24,64]{1,0,3,2:T(1,128)} %copy.368, s32[]{:T(128)S(6)} %sub.232, s32[]{:T(128)} %constant.126.clone.1..sunk.1, s32[]{:T(128)} %constant.126.clone.1..sunk.1, s32[]{:T(128)} %constant.126.clone.1..sunk.1) | dynamic-update-slice | bytes 3145732 | tf_op jit(solution)/shard_map/while/body/jit(dynamic_update_index_in_dim)/dynamic_update_slice | solution.py:153
  781.7 34.7 %dynamic_update_slice.76 = f32[4,256,24,64]{1,0,3,2:T(4,128)} dynamic-update-slice(f32[4,256,24,64]{1,0,3,2:T(4,128)} %get-tuple-element.941, f32[1,256,24,64]{1,0,3,2:T(1,128)} %copy.368, s32[]{:T(128)S(6)} %sub.232, s32[]{:T(128)} %constant.126.clone.1..sunk.1, s32[]{:T(128)} %constant.126.clone.1..sunk.1, s32[]{:T(128)} %constant.126.clone.1..sunk.1) | dynamic-update-slice | bytes 3145732 | tf_op jit(solution)/shard_map/while/body/jit(dynamic_update_index_in_dim)/dynamic_update_slice | solution.py:153
  842.8 19.0 %multiply_reduce_fusion.4 = (f32[1792]{0:T(1024)S(1)}, f32[1792]{0:T(1024)S(1)}, f32[1792]{0:T(1024)S(1)}, f32[1792]{0:T(1024)S(1)}, f32[1792]{0:T(1024)S(1)}, /*index=5*/f32[1024,1792]{0,1:T(8,128)S(1)}) fusion(f32[1024,1792]{0,1:T(8,128)} %copy-done.3, f32[1024,3352]{0,1:T(8,128)} %fusion.140, f32[1024,1792]{0,1:T(8,128)} %get-tuple-element.671, ...), kind=kLoop, calls=%fused_computation.169 | loop fusion | flops 36691200 | bytes 36736000 | tf_op jit(solution)/shard_map/transpose(jvp())/reduce_sum | solution.py:42
  870.4 12.1 fusion.103
  882.5 12.9 %fusion.119 = f32[768,3352]{1,0:T(8,128)} fusion(bf16[1024,768]{1,0:T(8,128)(2,1)S(1)} %copy-done.11, bf16[1024,24]{0,1:T(8,128)(2,1)S(1)} %get-tuple-element.665, bf16[1024,1792]{0,1:T(8,128)(2,1)} %fusion.103, bf16[1024,1536]{0,1:T(8,128)(2,1)} %get-tuple-element.688), kind=kOutput, calls=%fused_computation.210 | convolution fusion | flops 5292834816 | bytes 18735104 | tf_op jit(solution)/shard_map/ti,tj->ij/dot_general | solution.py:199
  907.9 11.7 reduce.22
  941.9 11.5 reduce.21
  954.8 20.8 %all-to-all-done.1 = bf16[16,2,24576]{2,1,0:T(2,128)(2,1)S(1)} async-done(((bf16[16,2,24576]{2,1,0:T(2,128)(2,1)}), bf16[16,2,24576]{2,1,0:T(2,128)(2,1)S(1)}, u32[]{:S(2)}, u32[]{:S(2)}) %all-to-all-start.1) | async-done | bytes 1572896 | tf_op jit(solution)/shard_map/all_to_all | solution.py:278
  975.5 27.4 %all-to-all-start.3 = ((bf16[16,2,24576]{2,1,0:T(2,128)(2,1)}), bf16[16,2,24576]{2,1,0:T(2,128)(2,1)S(1)}, u32[]{:S(2)}, u32[]{:S(2)}) async-start(bf16[16,2,24576]{2,1,0:T(2,128)(2,1)} %reshape.519), calls=%async_computation.3 | async-start | bytes 3145728 | tf_op jit(solution)/shard_map/all_to_all | solution.py:279
  1006.4 122.2 %reduce-scatter.6.cloned.1.call-done = f32[48,3352]{1,0:T(8,128)} async-done(((f32[768,3352]{1,0:T(8,128)}), f32[48,3352]{1,0:T(8,128)}) %reduce-scatter.6.cloned.1.call-update) | async-done | bytes 643600 | tf_op jit(solution)/shard_map/reduce_scatter | solution.py:296
  1128.9 75.2 %all-reduce.17 = (f32[768]{0:T(1024)S(1)}, f32[1792]{0:T(1024)S(1)}, f32[24]{0:T(128)S(1)}, f32[24]{0:T(128)S(1)}, f32[24]{0:T(128)S(1)}, /*index=5*/f32[1536]{0:T(1024)S(1)}) all-reduce(f32[768]{0:T(1024)S(1)} %get-tuple-element.592, f32[1792]{0:T(1024)S(1)} %get-tuple-element.590, ...), channel_id=2, replica_groups=mesh['rep'=2,'shard'=16] {'shard'}, use_global_device_ids=true, to_apply=%region_25.27.clone | all-reduce | flops 4168 | bytes 33344
  (443 shorter events, 395.2 us)
Async XLA Ops:
  7.2 240.9 %all-gather.4.cloned.1.call-start = ((), (), s32[]{:S(2)}) async-start(), calls=%async_computation.7 | async-start | bytes 5640192 | tf_op jit(solution)/shard_map/all_gather | solution.py:250
  12.6 73.9 %copy-start.43 = (u32[32]{0:T(128)S(1)}, u32[32]{0:T(128)}, u32[]{:S(2)}) copy-start(u32[32]{0:T(128)} %constant.162) | copy-start | bytes 388
  12.6 76.5 %copy-start.46 = (bf16[112]{0:T(256)(128)(2,1)S(1)}, bf16[112]{0:T(256)(128)(2,1)}, u32[]{:S(2)}) copy-start(bf16[112]{0:T(256)(128)(2,1)} %param.26) | copy-start | bytes 676
  12.6 76.7 %copy-start.47 = (bf16[96]{0:T(256)(128)(2,1)S(1)}, bf16[96]{0:T(256)(128)(2,1)}, u32[]{:S(2)}) copy-start(bf16[96]{0:T(256)(128)(2,1)} %param.30) | copy-start | bytes 580
  12.6 77.0 %copy-start.48 = (bf16[48]{0:T(256)(128)(2,1)S(1)}, bf16[48]{0:T(256)(128)(2,1)}, u32[]{:S(2)}) copy-start(bf16[48]{0:T(256)(128)(2,1)} %param.23) | copy-start | bytes 292
  12.6 193.1 %copy-start.44 = (bf16[112,4]{0,1:T(4,128)(2,1)S(1)}, bf16[112,4]{0,1:T(4,128)(2,1)}, u32[]{:S(2)}) copy-start(bf16[112,4]{0,1:T(4,128)(2,1)} %param.25) | copy-start | bytes 2692
  12.6 228.9 %copy-start.45 = (f32[24]{0:T(128)S(1)}, f32[24]{0:T(128)}, u32[]{:S(2)}) copy-start(f32[24]{0:T(128)} %param.29) | copy-start | bytes 292
  12.7 229.0 %copy-start.49 = (s32[1,16]{1,0:T(1,128)S(1)}, s32[1,16]{1,0:T(1,128)}, u32[]{:S(2)}) copy-start(s32[1,16]{1,0:T(1,128)} %param.21) | copy-start | bytes 196
  12.7 230.4 %copy-start.51 = (f32[24]{0:T(128)S(1)}, f32[24]{0:T(128)}, u32[]{:S(2)}) copy-start(f32[24]{0:T(128)} %param.28) | copy-start | bytes 292
  81.1 178.3 %copy-start.5 = (bf16[16,1,64,768]{3,2,1,0:T(8,128)(2,1)}, bf16[16,1,64,768]{3,2,1,0:T(8,128)(2,1)S(1)}, u32[]{:S(2)}) copy-start(bf16[16,1,64,768]{3,2,1,0:T(8,128)(2,1)S(1)} %all_to_all.42) | copy-start | bytes 4718596
  81.1 164.1 %all-to-all-start.2 = ((bf16[16,1,64,768]{3,2,1,0:T(8,128)(2,1)}), bf16[16,1,64,768]{3,2,1,0:T(8,128)(2,1)}, u32[]{:S(2)}, u32[]{:S(2)}) async-start(bf16[16,1,64,768]{3,2,1,0:T(8,128)(2,1)} %get-tuple-element.700), calls=%async_computation.2 | async-start | bytes 3145728 | tf_op jit(solution)/shard_map/all_to_all | solution.py:244
  85.6 413.4 %all-gather.6.cloned.1.call-start = ((), (), s32[]{:S(2)}) async-start(), calls=%async_computation.8 | async-start | bytes 2506752 | tf_op jit(solution)/shard_map/all_gather | solution.py:254
  86.4 920.0 %reduce-scatter.8.cloned.1.call-start = ((), (), s32[]{:S(2)}) async-start(), calls=%async_computation.10 | async-start | bytes 5013504 | tf_op jit(solution)/shard_map/reduce_scatter | solution.py:300
  205.8 53.7 %copy-start.25 = (f32[768]{0:T(1024)}, f32[768]{0:T(1024)S(1)}, u32[]{:S(2)}) copy-start(f32[768]{0:T(1024)S(1)} %convert_element_type.160) | copy-start | bytes 9220
  241.7 265.1 %copy-start.31 = (f32[1536]{0:T(1024)}, f32[1536]{0:T(1024)S(1)}, u32[]{:S(2)}) copy-start(f32[1536]{0:T(1024)S(1)} %convert_element_type.165) | copy-start | bytes 18436
  529.3 599.3 %reduce-scatter.6.cloned.1.call-start = ((), (), s32[]{:S(2)}) async-start(), calls=%async_computation.9 | async-start | bytes 11280384 | tf_op jit(solution)/shard_map/reduce_scatter | solution.py:296
  920.9 54.6 %all-to-all-start.1 = ((bf16[16,2,24576]{2,1,0:T(2,128)(2,1)}), bf16[16,2,24576]{2,1,0:T(2,128)(2,1)S(1)}, u32[]{:S(2)}, u32[]{:S(2)}) async-start(bf16[16,2,24576]{2,1,0:T(2,128)(2,1)} %reshape.517), calls=%async_computation.1 | async-start | bytes 3145728 | tf_op jit(solution)/shard_map/all_to_all | solution.py:278
  941.9 62.5 %copy-start.50 = (s32[1,16]{1,0:T(1,128)S(1)}, s32[1,16]{1,0:T(1,128)}, u32[]{:S(2)}) copy-start(s32[1,16]{1,0:T(1,128)} %param.22) | copy-start | bytes 196
  941.9 186.7 %copy-start.33 = (f32[1536]{0:T(1024)S(1)}, f32[1536]{0:T(1024)}, u32[]{:S(2)}) copy-start(f32[1536]{0:T(1024)} %get-tuple-element.662) | copy-start | bytes 18436
  941.9 186.9 %copy-start.52 = (f32[24]{0:T(128)S(1)}, f32[24]{0:T(128)}, u32[]{:S(2)}) copy-start(f32[24]{0:T(128)} %param.28) | copy-start | bytes 292
  941.9 187.0 %copy-start.38 = (f32[1536]{0:T(1024)S(1)}, f32[1536]{0:T(1024)}, u32[]{:S(2)}) copy-start(f32[1536]{0:T(1024)} %get-tuple-element.588) | copy-start | bytes 18436
  975.5 245.0 %all-to-all-start.3 = ((bf16[16,2,24576]{2,1,0:T(2,128)(2,1)}), bf16[16,2,24576]{2,1,0:T(2,128)(2,1)S(1)}, u32[]{:S(2)}, u32[]{:S(2)}) async-start(bf16[16,2,24576]{2,1,0:T(2,128)(2,1)} %reshape.519), calls=%async_computation.3 | async-start | bytes 3145728 | tf_op jit(solution)/shard_map/all_to_all | solution.py:279
  1002.9 205.3 %reduce-scatter.10.cloned.1.call-start = ((), (), s32[]{:S(2)}) async-start(), calls=%async_computation.11 | async-start | bytes 974848
  1004.3 233.0 %all-reduce.23.cloned.1.call-start = ((), (), s32[]{:S(2)}) async-start(), calls=%async_computation.12 | async-start | bytes 1916928 | tf_op jit(solution)/shard_map/psum | solution.py:283
  (38 other events, 451.4 us)
Sparse Core Ops, SparseCore 0:
  10.8 132.4 all-gather.3
  146.1 62.0 all-gather.5
  529.4 135.1 reduce-scatter.7
  895.6 232.9 reduce-scatter.5
  1131.3 76.8 reduce-scatter.9
  1210.6 15.8 all-reduce.22
